TPU v7x, 32 devices: a whole 2x2x4 slice. The times are simulated.
32 devices in a mesh: group: 2 (over x), src: 16 (over z, y, core).
Axes of the slice: x: 2, y: 2, z: 4, core: 2. Of those that a mesh axis runs over, the one named last changes fastest.
Arguments:
- rcv_points: float32 [3, 4096], P(None, ('group', 'src')), parts along dimension 1, may hold values from -1 to 1
- rcv_normals: float32 [3, 4096], P(None, ('group', 'src')), parts along dimension 1, may hold values from -4 to 4
- left_modes: float32 [8, 4096], P(None, ('group', 'src')), parts along dimension 1, may hold values from -5 to 5
- vertices: float32 [3, 2048], P(None, ('group', 'src')), parts along dimension 1, may hold values from -1 to 1
- connect: int32 [2, 4096], P(None, ('group', 'src')), parts along dimension 1, may hold values from 0 to 1023, as said below
- right_modes: float32 [8, 4096], P(None, ('group', 'src')), parts along dimension 1, may hold values from -0.125 to 0.125
- mode_weights: float32 [16], P('group'), parts along dimension 0, may hold values from 0.25 to 1
Outputs:
- rcv_grad: float32 [6, 4096], P(None, ('group', 'src')), parts along dimension 1
- vert_grad: float32 [3, 2048], P(None, ('group', 'src')), parts along dimension 1
There are 2 independent parts, one for each index of `group`. A program takes and returns all parts, laid end to end along the dimension named above; each array names one. Nothing has to cross between parts.
Inputs may be any that keep to these rules, and one draw needn't show every extreme that they name: `connect`: a panel's first vertex is one of the 64 vertices held at the same index of src as the panel, and its second vertex is the next vertex number.
All inputs are finite; a program needn't handle non-finite values.
Results may differ from a plain program's by a relative error of at most 0.0003.
Values sent between devices are 32-bit elements; how exact they have to be, the bound alone decides.
No kernel may reach another device: no remote copies, remote signals or barrier semaphores. Data moves between devices by JAX's collectives and lax.ppermute only.
A program may use at most 64 MiB of HBM per device.

v0:
```python
import math
import jax
import jax.numpy as jnp
from jax import lax
from jax.sharding import PartitionSpec as P

core_term = 0.05
inverse_four_pi = 0.25 / math.pi


def shifted(value, axis, steps):
    count = lax.axis_size(axis)
    leading, last = (max(0, -steps), min(count, count - steps))
    return lax.ppermute(value, axis, [(source, source + steps) for source in range(leading, last)])


def lift_points(raw):
    return jnp.stack([raw[0], raw[1], 0.5 + 0.2 * raw[2]])


def place_points(raw):
    return jnp.stack([raw[0], raw[1], 0.2 * raw[2]])


def tile_energy(points, normals, first_end, second_end, coefficient):
    rel_first = points[:, None, :] - first_end[:, :, None]
    rel_second = points[:, None, :] - second_end[:, :, None]
    segment = (second_end - first_end)[:, :, None]
    cross_x = rel_first[1] * rel_second[2] - rel_first[2] * rel_second[1]
    cross_y = rel_first[2] * rel_second[0] - rel_first[0] * rel_second[2]
    cross_z = rel_first[0] * rel_second[1] - rel_first[1] * rel_second[0]
    cross_sq = cross_x * cross_x + cross_y * cross_y + cross_z * cross_z
    dist_first = jnp.sqrt(jnp.sum(rel_first * rel_first, axis=0))
    dist_second = jnp.sqrt(jnp.sum(rel_second * rel_second, axis=0))
    along_term = jnp.sum(segment * (rel_first / dist_first - rel_second / dist_second), axis=0)
    span_sq = jnp.sum(segment * segment, axis=0)
    denominator = cross_sq + core_term * (span_sq + 1.0)
    normal_term = (
        normals[0][None, :] * cross_x
        + normals[1][None, :] * cross_y
        + normals[2][None, :] * cross_z
    )
    influence = inverse_four_pi * normal_term * along_term / denominator
    return jnp.sum(coefficient * influence)


def tile_gradients(points, normals, first_end, second_end, coefficient):
    return jax.grad(tile_energy, argnums=(0, 1, 2, 3))(
        points, normals, first_end, second_end, coefficient
    )


def on_device(rcv_points, rcv_normals, left_modes, vertices, connect, right_modes, mode_weights):
    own_count = vertices.shape[1]
    next_first = shifted(vertices[:, :1], "src", -1)
    extended = jnp.concatenate([vertices, next_first], axis=1)
    places = place_points(extended)
    base_vertex = lax.axis_index("src") * own_count
    local_first = connect[0] - base_vertex
    local_second = local_first + 1
    first_end = places[:, local_first]
    second_end = places[:, local_second]
    points = lift_points(rcv_points)
    chain_scale = jnp.array([1.0, 1.0, 0.2], dtype=jnp.float32)[:, None]
    weighted = right_modes * mode_weights[:, None]
    receiver_count = rcv_points.shape[1] * lax.axis_size("src")
    source_count = connect.shape[1]
    start_totals = (
        jnp.zeros((3, source_count), jnp.float32),
        jnp.zeros((3, source_count), jnp.float32),
        jnp.zeros((6, receiver_count), jnp.float32),
    )
    shard_points = lax.all_gather(points, "src", axis=1, tiled=True)
    shard_normals = lax.all_gather(rcv_normals, "src", axis=1, tiled=True)
    shard_left = lax.all_gather(left_modes, "src", axis=1, tiled=True)
    row_count = shard_points.shape[1]
    width_rows = math.gcd(row_count, 2048)

    def advance(number, inner):
        sum_first, sum_second, receiver_buffer = inner
        local_start = number * width_rows
        block_points = lax.dynamic_slice_in_dim(shard_points, local_start, width_rows, 1)
        block_normals = lax.dynamic_slice_in_dim(shard_normals, local_start, width_rows, 1)
        block_left = lax.dynamic_slice_in_dim(shard_left, local_start, width_rows, 1)
        coefficient = jnp.einsum("mj,mi->ji", weighted, block_left, precision=lax.Precision.HIGHEST)
        grads = tile_gradients(block_points, block_normals, first_end, second_end, coefficient)
        rows_out = jnp.concatenate([grads[0] * chain_scale, grads[1]], axis=0)
        receiver_buffer = lax.dynamic_update_slice_in_dim(receiver_buffer, rows_out, local_start, 1)
        return (sum_first + grads[2], sum_second + grads[3], receiver_buffer)

    sum_first, sum_second, receiver_buffer = lax.fori_loop(
        0, row_count // width_rows, advance, start_totals
    )
    rcv_grad = lax.psum_scatter(receiver_buffer, "src", scatter_dimension=1, tiled=True)
    vertex_partial = jnp.zeros((3, own_count + 1), jnp.float32)
    vertex_partial = (
        vertex_partial.at[:, local_first].add(sum_first).at[:, local_second].add(sum_second)
    )
    incoming = shifted(vertex_partial[:, own_count:], "src", 1)
    own_part = vertex_partial[:, :own_count]
    own_part = jnp.concatenate([own_part[:, :1] + incoming, own_part[:, 1:]], axis=1)
    vert_grad = own_part * chain_scale
    return (rcv_grad, vert_grad)


def solution(mesh):
    in_specs = (
        P(None, ("group", "src")),
        P(None, ("group", "src")),
        P(None, ("group", "src")),
        P(None, ("group", "src")),
        P(None, ("group", "src")),
        P(None, ("group", "src")),
        P("group"),
    )
    out_specs = (P(None, ("group", "src")), P(None, ("group", "src")))
    return jax.shard_map(
        on_device, mesh=mesh, in_specs=in_specs, out_specs=out_specs, check_vma=False
    )
```

profile of v0, /device:TPU:0, one launch (start us, length us, event | category | flops | bytes accessed | tf_op | source)
XLA Modules:
  0.0 154.4 jit_solution(849035136935577808)
XLA Ops:
  7.2 0.0 reduce-scatter.2.cloned.1.call-start
  7.2 1.3 collective-permute-start
  8.5 0.7 multiply_add_fusion.1
  9.2 0.7 slice.81
  9.9 23.8 %all_gather.10 = f32[3,2048]{1,0:T(4,128)S(1)} all-gather(f32[3,128]{1,0:T(4,128)S(1)} %pad_maximum_fusion.3), channel_id=1, replica_groups=mesh['group'=2,'src'=16] {'src'}, dimensions={1}, use_global_device_ids=true | all-gather | bytes 26112 | tf_op jit(solution)/shard_map/all_gather | solution.py:73
  33.7 17.7 %all_gather.9 = f32[3,2048]{1,0:T(4,128)S(1)} all-gather(f32[3,128]{1,0:T(4,128)} %param.9), channel_id=1, replica_groups=mesh['group'=2,'src'=16] {'src'}, dimensions={1}, use_global_device_ids=true | all-gather | bytes 26112 | tf_op jit(solution)/shard_map/all_gather | solution.py:74
  51.4 19.2 %all_gather.11 = f32[8,2048]{1,0:T(8,128)S(1)} all-gather(f32[8,128]{1,0:T(8,128)} %param.10), channel_id=1, replica_groups=mesh['group'=2,'src'=16] {'src'}, dimensions={1}, use_global_device_ids=true | all-gather | bytes 69632 | tf_op jit(solution)/shard_map/all_gather | solution.py:75
  70.6 0.7 fusion.24
  71.3 0.0 collective-permute-done
  71.3 0.8 pad_maximum_fusion.1
  72.1 0.1 copy.26
  72.2 0.6 gather_fusion.1
  72.9 0.1 copy.29
  72.9 0.7 gather_fusion
  73.6 0.1 copy.27
  73.7 0.8 fusion.15
  74.5 0.0 copy-start.2
  74.5 0.0 copy-start.3
  74.6 0.3 multiply_divide_fusion.1
  74.9 0.3 multiply_divide_fusion.2
  75.3 0.0 copy-done.2
  75.3 0.0 copy-done.3
  75.3 1.8 %divide_multiply_fusion.1 = (f32[128,2048]{1,0:T(8,128)S(1)}, f32[128,2048]{1,0:T(8,128)S(1)}, f32[128,2048]{1,0:T(8,128)S(1)}, f32[128,2048]{1,0:T(8,128)S(1)},...) fusion(f32[128]{0:T(128)S(1)} %add_multiply_fusion.2, f32[2048]{0:T(1024)S(1)} %bitcast.136, ...), kind=kOutput, calls=%fused_computation.109 | convolution fusion | flops 31196160 | bytes 13726240 | tf_op jit(solution)/shard_map/while/body/eval_jaxpr/mj,mi->ji/dot_general | solution.py:85
  77.1 2.5 %multiply_reduce_fusion = (f32[3,128]{1,0:T(4,128)S(1)}, f32[128,2048]{1,0:T(8,128)S(1)}, f32[128,2048]{1,0:T(8,128)S(1)}, f32[128,2048]{1,0:T(8,128)S(1)}) fusion(f32[128,2048]{1,0:T(8,128)S(1)} %get-tuple-element.62, f32[128,2048]{1,0:T(8,128)S(1)} %get-tuple-element.92, f32[3,128]{1,0:T(4,128)S(1)} %bitcast.127, f32[128,2048]{1,0:T(8,128)S(1)} %get-tuple-element.94, ...), kind=kLoop, calls=%fused_computation.36 | loop fusion | flops 12582528 | bytes 8419328 | tf_op jit(solution)/shard_map/while/body/eval_jaxpr/transpose(jvp())/reduce_sum | solution.py:35
  79.6 0.2 multiply_multiply_fusion.3
  79.8 0.2 multiply_multiply_fusion.1
  80.1 0.6 fusion.28
  80.6 2.0 %multiply_bitcast_fusion.5 = (f32[1,128,2048]{2,1,0:T(8,128)}, f32[128,2048]{1,0:T(8,128)}, f32[128,2048]{1,0:T(8,128)S(1)}) fusion(f32[3,128,2048]{2,1,0:T(8,128)S(1)} %get-tuple-element.95, f32[128,2048]{1,0:T(8,128)S(1)} %get-tuple-element.67, f32[128,2048]{1,0:T(8,128)S(1)} %get-tuple-element.54, f32[2048]{0:T(1024)S(1)} %broadcast_multiply_fusion.2, ...), kind=kLoop, calls=%fused_computation.57 | loop fusion | flops 2359296 | bytes 9445376 | tf_op jit(solution)/shard_map/while/body/eval_jaxpr/transpose(jvp())/broadcast_in_dim | solution.py:31
  82.6 2.2 %multiply_bitcast_fusion.3 = (f32[1,128,2048]{2,1,0:T(8,128)S(1)}, f32[128,2048]{1,0:T(8,128)}, f32[1,128,2048]{2,1,0:T(8,128)S(1)}, f32[128,2048]{1,0:T(8,128)}...) fusion(f32[3,128,2048]{2,1,0:T(8,128)S(1)} %get-tuple-element.95, f32[128,2048]{1,0:T(8,128)S(1)} %get-tuple-element.66, ...), kind=kLoop, calls=%fused_computation.55 | loop fusion | flops 5236736 | bytes 11575296 | tf_op jit(solution)/shard_map/while/body/eval_jaxpr/transpose(jvp())/broadcast_in_dim | solution.py:30
  84.9 4.8 %multiply_bitcast_fusion.11 = (f32[1,128,2048]{2,1,0:T(8,128)S(1)}, f32[1,128,2048]{2,1,0:T(8,128)S(1)}, f32[1,128,2048]{2,1,0:T(8,128)S(1)}, f32[1,128,2048]{2,...) fusion(f32[128,2048]{1,0:T(8,128)} %get-tuple-element.56, ...), kind=kLoop, calls=%fused_computation.65 | loop fusion | flops 3145728 | bytes 18874368 | tf_op jit(solution)/shard_map/while/body/eval_jaxpr/transpose(jvp())/broadcast_in_dim | solution.py:31
  89.7 3.4 %fusion.27 = (f32[3,128]{1,0:T(4,128)S(1)}, f32[3,2048]{1,0:T(4,128)S(1)}) fusion(f32[1,128,2048]{2,1,0:T(8,128)} %get-tuple-element.88, f32[1,128,2048]{2,1,0:T(8,128)S(1)} %get-tuple-element.70, f32[1,128,2048]{2,1,0:T(8,128)} %get-tuple-element.89, f32[1,128,2048]{2,1,0:T(8,128)S(1)} %get-tuple-element.58, f32[1,128,2048]{2,1,0:T(8,128)} %get-tuple-element.90, ...), kind=kLoop, calls=%fused_computation.111 | loop fusion | flops 11003520 | bytes 9490944 | tf_op jit(solution)/shard_map/while/body/eval_jaxpr/transpose(jvp())/reduce_sum | solution.py:26
  93.1 0.0 copy-done
  93.1 0.0 copy-start.1
  93.1 1.9 %fusion.26 = (f32[3,128]{1,0:T(4,128)S(1)}, f32[3,2048]{1,0:T(4,128)S(1)}) fusion(f32[1,128,2048]{2,1,0:T(8,128)S(1)} %get-tuple-element.84, f32[1,128,2048]{2,1,0:T(8,128)S(1)} %get-tuple-element.85, f32[1,128,2048]{2,1,0:T(8,128)S(1)} %get-tuple-element.86, f32[1,128,2048]{2,1,0:T(8,128)S(1)} %copy-done, f32[1,128,2048]{2,1,0:T(8,128)S(1)} %get-tuple-element.73, ...), kind=kLoop, calls=%fused_computation.110 | loop fusion | flops 11789952 | bytes 9490944 | tf_op jit(solution)/shard_map/while/body/eval_jaxpr/transpose(jvp())/reduce_sum | solution.py:27
  95.0 0.1 copy.31
  95.1 0.1 copy.30
  95.2 1.0 scatter_custom_fusion
  96.2 1.2 scatter_fusion
  97.5 0.0 copy-done.1
  97.5 0.1 add_multiply_fusion.1
  97.6 0.6 pad_maximum_fusion
  98.2 0.0 reduce-scatter.2.cloned.1.call-update
  98.3 2.2 %collective-permute-start.1 = (f32[3,1]{0,1:T(1,128)S(1)}, f32[3,1]{0,1:T(1,128)S(1)}, u32[]{:S(2)}, u32[]{:S(2)}) collective-permute-start(f32[3,1]{0,1:T(1,128)S(1)} %slice.108), channel_id=1, source_target_pairs={{0,1},{1,2},{2,3},{3,4},{4,5},{5,6},{6,7},{7,8},{8,9},{9,10},{10,1... | collective-permute-start | bytes 44 | tf_op jit(solution)/shard_map/ppermute | solution.py:14
  100.5 0.1 copy.33
  100.6 0.7 collective-permute-done.1
  101.3 0.1 copy.32
  101.4 0.7 maximum_multiply_fusion
  102.1 45.5 %reduce-scatter.2.cloned.1.call-done = f32[6,128]{1,0:T(8,128)} async-done(((f32[6,2048]{1,0:T(8,128)}), f32[6,128]{1,0:T(8,128)}) %reduce-scatter.2.cloned.1.call-update) | async-done | bytes 3088 | tf_op jit(solution)/shard_map/reduce_scatter | solution.py:94
  (17 shorter events, 0.2 us)
Async XLA Ops:
  7.2 140.4 %reduce-scatter.2.cloned.1.call-start = ((), (), s32[]{:S(2)}) async-start(), calls=%async_computation.1 | async-start | bytes 69632 | tf_op jit(solution)/shard_map/reduce_scatter | solution.py:94
  7.2 64.1 %collective-permute-start = (f32[3,1]{1,0:T(4,128)}, f32[3,1]{1,0:T(4,128)S(1)}, u32[]{:S(2)}, u32[]{:S(2)}) collective-permute-start(f32[3,1]{1,0:T(4,128)} %bitcast.141), channel_id=1, source_target_pairs={{1,0},{2,1},{3,2},{4,3},{5,4},{6,5},{7,6},{8,7},{9,8},{10,9},{11,1... | collective-permute-start | bytes 44 | tf_op jit(solution)/shard_map/ppermute | solution.py:14
  74.5 0.7 copy-start.2
  74.5 0.7 copy-start.3
  89.7 3.4 %copy-start = (f32[1,128,2048]{2,1,0:T(8,128)S(1)}, f32[1,128,2048]{2,1,0:T(8,128)}, u32[]{:S(2)}) copy-start(f32[1,128,2048]{2,1,0:T(8,128)} %get-tuple-element.87) | copy-start | bytes 3145732
  93.1 4.4 %copy-start.1 = (f32[3]{0:T(128)S(1)}, f32[3]{0:T(128)}, u32[]{:S(2)}) copy-start(f32[3]{0:T(128)} %constant.34.clone) | copy-start | bytes 40
  98.3 3.1 %collective-permute-start.1 = (f32[3,1]{0,1:T(1,128)S(1)}, f32[3,1]{0,1:T(1,128)S(1)}, u32[]{:S(2)}, u32[]{:S(2)}) collective-permute-start(f32[3,1]{0,1:T(1,128)S(1)} %slice.108), channel_id=1, source_target_pairs={{0,1},{1,2},{2,3},{3,4},{4,5},{5,6},{6,7},{7,8},{8,9},{9,10},{10,1... | collective-permute-start | bytes 44 | tf_op jit(solution)/shard_map/ppermute | solution.py:14
Sparse Core Ops, SparseCore 0:
  98.4 49.1 reduce-scatter.1
where the time goes:
time: 155 us; the launch traced here: 154 us
  blocking collectives  60.7 us (39%)
  waiting for transfers between devices  46.3 us (30%)
  other arithmetic  25.1 us (16%)
  between operations  14.3 us (9%)
  starting transfers between devices  3.57 us (2%)
  local copies, waits for them, and re-layouts  2.68 us (2%)
  matrix products  1.85 us (1%)
    reduce_scatter x1, waiting for transfers between devices, on_device(): lax.psum_scatter(receiver_buffer, 'src', scatter_dimension=1, tiled=True)  45.5 us
    all_gather x1, blocking collectives, on_device(): shard_points = lax.all_gather(points, 'src', axis=1, tiled=True)  23.8 us
    all_gather x1, blocking collectives, on_device(): shard_left = lax.all_gather(left_modes, 'src', axis=1, tiled=True)  19.2 us
    all_gather x1, blocking collectives, on_device(): shard_normals = lax.all_gather(rcv_normals, 'src', axis=1, tiled=True)  17.7 us
    broadcast_in_dim x2, other arithmetic, tile_energy(): cross_z = rel_first[0] * rel_second[1] - rel_first[1] * rel_second[0]  6.79 us
    ppermute x2, starting transfers between devices, shifted(): lax.ppermute(value, axis, [(source, source + steps) for source in range(l...  3.54 us
    reduce_sum x1, other arithmetic, tile_energy(): rel_first = points[:, None, :] - first_end[:, :, None]  3.41 us
  transfers between devices with their start and end apart: 3, of which 2 were waited for; matrix products, arithmetic and copies ran while one was open for 2% of the time, Pallas kernels for 0%

commit v1 on v0

--- a/solution.py
+++ b/solution.py
@@ -6,6 +6,21 @@
 
 core_term = 0.05
 inverse_four_pi = 0.25 / math.pi
+
+
+def stocks_edit(here_x):
+    taken_in = lax.axis_size("src")
+    arr_next, newest = (taken_in, lax.axis_index("src"))
+    out_arr, v1 = (here_x, 1)
+    while v1 < arr_next:
+        reached = lax.ppermute(
+            out_arr, "src", list(map(lambda hop_no: (hop_no, hop_no ^ v1), range(arr_next)))
+        )
+        then = jnp.concatenate([out_arr, reached], axis=1)
+        new = jnp.concatenate([reached, out_arr], axis=1)
+        out_arr = jnp.where(newest & v1 == 0, then, new)
+        v1 = 2 * v1
+    return out_arr
 
 
 def shifted(value, axis, steps):
@@ -70,7 +85,7 @@
         jnp.zeros((3, source_count), jnp.float32),
         jnp.zeros((6, receiver_count), jnp.float32),
     )
-    shard_points = lax.all_gather(points, "src", axis=1, tiled=True)
+    shard_points = stocks_edit(points)
     shard_normals = lax.all_gather(rcv_normals, "src", axis=1, tiled=True)
     shard_left = lax.all_gather(left_modes, "src", axis=1, tiled=True)
     row_count = shard_points.shape[1]

time: 155 us -> 148 us (0.955)
  blocking collectives: 60.7 us -> 42.1 us
  waiting for transfers between devices: 46.3 us -> 57 us
    all_gather x1 -> x0, blocking collectives: 23.8 us -> none  [on_device(): shard_points = lax.all_gather(points, 'src', axis=1, tiled=True)]
    ppermute x0 -> x4, waiting for transfers between devices: none -> 8.68 us  [stocks_edit(): lax.ppermute(out_arr, 'src', list(map(lambda hop_no: (hop_no, hop_no ^ v1...]
    all_gather x1, blocking collectives: 17.7 us -> 24.2 us  [on_device(): shard_normals = lax.all_gather(rcv_normals, 'src', axis=1, tiled=True)]
    ppermute x0 -> x4, starting transfers between devices: none -> 2.14 us  [stocks_edit(): lax.ppermute(out_arr, 'src', list(map(lambda hop_no: (hop_no, hop_no ^ v1...]
    reduce_scatter x1, waiting for transfers between devices: 45.5 us -> 47.5 us  [on_device(): lax.psum_scatter(receiver_buffer, 'src', scatter_dimension=1, tiled=True)]
  transfers between devices with their start and end apart: 3 -> 7, of which waited for: 2 -> 5; matrix products, arithmetic and copies ran while one was open for 2% -> 3% of each run, Pallas kernels for 0% -> 0%
where the time goes in v1:
time: 148 us
  waiting for transfers between devices  57 us (39%)
  blocking collectives  42.1 us (28%)
  other arithmetic  25.2 us (17%)
  between operations  14.3 us (10%)
  starting transfers between devices  4.75 us (3%)
  local copies, waits for them, and re-layouts  2.68 us (2%)
  matrix products  1.86 us (1%)
    reduce_scatter x1, waiting for transfers between devices, on_device(): lax.psum_scatter(receiver_buffer, 'src', scatter_dimension=1, tiled=True)  47.5 us
    all_gather x1, blocking collectives, on_device(): shard_normals = lax.all_gather(rcv_normals, 'src', axis=1, tiled=True)  24.2 us
    all_gather x1, blocking collectives, on_device(): shard_left = lax.all_gather(left_modes, 'src', axis=1, tiled=True)  17.9 us
    ppermute x4, waiting for transfers between devices, stocks_edit(): lax.ppermute(out_arr, 'src', list(map(lambda hop_no: (hop_no, hop_no ^ v1...  8.68 us
    broadcast_in_dim x2, other arithmetic, tile_energy(): cross_z = rel_first[0] * rel_second[1] - rel_first[1] * rel_second[0]  6.79 us
    reduce_sum x1, other arithmetic, tile_energy(): rel_first = points[:, None, :] - first_end[:, :, None]  3.41 us
  transfers between devices with their start and end apart: 7, of which 5 were waited for; matrix products, arithmetic and copies ran while one was open for 3% of the time, Pallas kernels for 0%

profile of v1, /device:TPU:0, one launch (start us, length us, event | category | flops | bytes accessed | tf_op | source)
XLA Modules:
  0.0 147.8 jit_solution(16479198596927734575)
XLA Ops:
  7.2 0.0 reduce-scatter.2.cloned.1.call-start
  7.2 0.7 multiply_add_fusion.1
  7.9 0.7 slice.81
  8.6 0.5 collective-permute-start.1
  9.0 1.3 collective-permute-start
  10.3 24.2 %all_gather.6 = f32[3,2048]{1,0:T(4,128)S(1)} all-gather(f32[3,128]{1,0:T(4,128)} %param.9), channel_id=1, replica_groups=mesh['group'=2,'src'=16] {'src'}, dimensions={1}, use_global_device_ids=true | all-gather | bytes 26112 | tf_op jit(solution)/shard_map/all_gather | solution.py:89
  34.6 17.9 %all_gather.7 = f32[8,2048]{1,0:T(8,128)S(1)} all-gather(f32[8,128]{1,0:T(8,128)} %param.10), channel_id=1, replica_groups=mesh['group'=2,'src'=16] {'src'}, dimensions={1}, use_global_device_ids=true | all-gather | bytes 69632 | tf_op jit(solution)/shard_map/all_gather | solution.py:90
  52.5 0.7 fusion.24
  53.2 0.8 pad_maximum_fusion.1
  54.0 0.0 collective-permute-done.1
  54.0 1.7 %collective-permute-start.2 = (f32[3,256]{1,0:T(4,128)S(1)}, f32[3,256]{1,0:T(4,128)S(1)}, u32[]{:S(2)}, u32[]{:S(2)}) collective-permute-start(f32[3,256]{1,0:T(4,128)S(1)} %maximum_select_fusion.3), channel_id=1, source_target_pairs={{0,2},{1,3},{2,0},{3,1},{4,6},{5,7},{6,4},{7,5},{8,10},{9,11},{10,... | collective-permute-start | bytes 9224 | tf_op jit(solution)/shard_map/ppermute | solution.py:16
  55.7 0.1 copy.26
  55.8 0.6 gather_fusion.1
  56.4 0.1 copy.29
  56.5 0.7 gather_fusion
  57.2 0.1 copy.27
  57.2 0.4 collective-permute-done.2
  57.7 3.6 %collective-permute-done.3 = f32[3,512]{1,0:T(4,128)S(1)} collective-permute-done((f32[3,512]{1,0:T(4,128)S(1)}, f32[3,512]{1,0:T(4,128)S(1)}, u32[]{:S(2)}, u32[]{:S(2)}) %collective-permute-start.3) | collective-permute-done | bytes 6176 | tf_op jit(solution)/shard_map/ppermute | solution.py:16
  61.3 4.6 %collective-permute-done.4 = f32[3,1024]{1,0:T(4,128)S(1)} collective-permute-done((f32[3,1024]{1,0:T(4,128)S(1)}, f32[3,1024]{1,0:T(4,128)S(1)}, u32[]{:S(2)}, u32[]{:S(2)}) %collective-permute-start.4) | collective-permute-done | bytes 12320 | tf_op jit(solution)/shard_map/ppermute | solution.py:16
  66.0 0.8 fusion.15
  66.8 0.0 copy-start.2
  66.8 0.0 copy-start.3
  66.8 0.3 multiply_divide_fusion.1
  67.2 0.3 multiply_divide_fusion.2
  67.5 1.9 %divide_multiply_fusion.1 = (f32[128,2048]{1,0:T(8,128)S(1)}, f32[128,2048]{1,0:T(8,128)S(1)}, f32[128,2048]{1,0:T(8,128)S(1)}, f32[128,2048]{1,0:T(8,128)S(1)},...) fusion(f32[128]{0:T(128)S(1)} %add_multiply_fusion.2, f32[2048]{0:T(1024)S(1)} %bitcast.136, ...), kind=kOutput, calls=%fused_computation.113 | convolution fusion | flops 31196160 | bytes 13726240 | tf_op jit(solution)/shard_map/while/body/eval_jaxpr/mj,mi->ji/dot_general | solution.py:100
  69.4 2.5 %multiply_reduce_fusion = (f32[3,128]{1,0:T(4,128)S(1)}, f32[128,2048]{1,0:T(8,128)S(1)}, f32[128,2048]{1,0:T(8,128)S(1)}, f32[128,2048]{1,0:T(8,128)S(1)}) fusion(f32[128,2048]{1,0:T(8,128)S(1)} %get-tuple-element.62, f32[128,2048]{1,0:T(8,128)S(1)} %get-tuple-element.92, f32[3,128]{1,0:T(4,128)S(1)} %bitcast.127, f32[128,2048]{1,0:T(8,128)S(1)} %get-tuple-element.94, ...), kind=kLoop, calls=%fused_computation.36 | loop fusion | flops 12582528 | bytes 8419328 | tf_op jit(solution)/shard_map/while/body/eval_jaxpr/transpose(jvp())/reduce_sum | solution.py:50
  71.9 0.2 multiply_multiply_fusion.3
  72.1 0.2 multiply_multiply_fusion.1
  72.3 0.6 fusion.28
  72.9 2.0 %multiply_bitcast_fusion.5 = (f32[1,128,2048]{2,1,0:T(8,128)}, f32[128,2048]{1,0:T(8,128)}, f32[128,2048]{1,0:T(8,128)S(1)}) fusion(f32[3,128,2048]{2,1,0:T(8,128)S(1)} %get-tuple-element.95, f32[128,2048]{1,0:T(8,128)S(1)} %get-tuple-element.67, f32[128,2048]{1,0:T(8,128)S(1)} %get-tuple-element.54, f32[2048]{0:T(1024)S(1)} %broadcast_multiply_fusion.2, ...), kind=kLoop, calls=%fused_computation.57 | loop fusion | flops 2359296 | bytes 9445376 | tf_op jit(solution)/shard_map/while/body/eval_jaxpr/transpose(jvp())/broadcast_in_dim | solution.py:46
  74.9 2.2 %multiply_bitcast_fusion.3 = (f32[1,128,2048]{2,1,0:T(8,128)S(1)}, f32[128,2048]{1,0:T(8,128)}, f32[1,128,2048]{2,1,0:T(8,128)S(1)}, f32[128,2048]{1,0:T(8,128)}...) fusion(f32[3,128,2048]{2,1,0:T(8,128)S(1)} %get-tuple-element.95, f32[128,2048]{1,0:T(8,128)S(1)} %get-tuple-element.66, ...), kind=kLoop, calls=%fused_computation.55 | loop fusion | flops 5236736 | bytes 11575296 | tf_op jit(solution)/shard_map/while/body/eval_jaxpr/transpose(jvp())/broadcast_in_dim | solution.py:45
  77.1 4.8 %multiply_bitcast_fusion.11 = (f32[1,128,2048]{2,1,0:T(8,128)S(1)}, f32[1,128,2048]{2,1,0:T(8,128)S(1)}, f32[1,128,2048]{2,1,0:T(8,128)S(1)}, f32[1,128,2048]{2,...) fusion(f32[128,2048]{1,0:T(8,128)} %get-tuple-element.56, ...), kind=kLoop, calls=%fused_computation.65 | loop fusion | flops 3145728 | bytes 18874368 | tf_op jit(solution)/shard_map/while/body/eval_jaxpr/transpose(jvp())/broadcast_in_dim | solution.py:46
  81.9 3.4 %fusion.27 = (f32[3,128]{1,0:T(4,128)S(1)}, f32[3,2048]{1,0:T(4,128)S(1)}) fusion(f32[1,128,2048]{2,1,0:T(8,128)} %get-tuple-element.88, f32[1,128,2048]{2,1,0:T(8,128)S(1)} %get-tuple-element.70, f32[1,128,2048]{2,1,0:T(8,128)} %get-tuple-element.89, f32[1,128,2048]{2,1,0:T(8,128)S(1)} %get-tuple-element.58, f32[1,128,2048]{2,1,0:T(8,128)} %get-tuple-element.90, ...), kind=kLoop, calls=%fused_computation.115 | loop fusion | flops 11003520 | bytes 9490944 | tf_op jit(solution)/shard_map/while/body/eval_jaxpr/transpose(jvp())/reduce_sum | solution.py:41
  85.4 0.0 copy-start.1
  85.4 1.9 %fusion.26 = (f32[3,128]{1,0:T(4,128)S(1)}, f32[3,2048]{1,0:T(4,128)S(1)}) fusion(f32[1,128,2048]{2,1,0:T(8,128)S(1)} %get-tuple-element.84, f32[1,128,2048]{2,1,0:T(8,128)S(1)} %get-tuple-element.85, f32[1,128,2048]{2,1,0:T(8,128)S(1)} %get-tuple-element.86, f32[1,128,2048]{2,1,0:T(8,128)S(1)} %copy-done, f32[1,128,2048]{2,1,0:T(8,128)S(1)} %get-tuple-element.73, ...), kind=kLoop, calls=%fused_computation.114 | loop fusion | flops 11789952 | bytes 9490944 | tf_op jit(solution)/shard_map/while/body/eval_jaxpr/transpose(jvp())/reduce_sum | solution.py:42
  87.3 0.1 copy.31
  87.4 0.1 copy.30
  87.5 1.0 scatter_custom_fusion
  88.5 1.2 scatter_fusion
  89.8 0.1 add_multiply_fusion.1
  89.9 0.6 pad_maximum_fusion
  90.5 0.0 reduce-scatter.2.cloned.1.call-update
  90.5 1.3 collective-permute-start.5
  91.8 0.1 copy.33
  91.9 0.7 collective-permute-done.5
  92.6 0.1 copy.32
  92.7 0.7 maximum_multiply_fusion
  93.4 47.5 %reduce-scatter.2.cloned.1.call-done = f32[6,128]{1,0:T(8,128)} async-done(((f32[6,2048]{1,0:T(8,128)}), f32[6,128]{1,0:T(8,128)}) %reduce-scatter.2.cloned.1.call-update) | async-done | bytes 3088 | tf_op jit(solution)/shard_map/reduce_scatter | solution.py:109
  (28 shorter events, 0.2 us)
Async XLA Ops:
  7.2 133.8 %reduce-scatter.2.cloned.1.call-start = ((), (), s32[]{:S(2)}) async-start(), calls=%async_computation.1 | async-start | bytes 69632 | tf_op jit(solution)/shard_map/reduce_scatter | solution.py:109
  8.6 45.4 %collective-permute-start.1 = (f32[3,128]{1,0:T(4,128)S(1)}, f32[3,128]{1,0:T(4,128)S(1)}, u32[]{:S(2)}, u32[]{:S(2)}) collective-permute-start(f32[3,128]{1,0:T(4,128)S(1)} %pad_maximum_fusion.3), channel_id=1, source_target_pairs={{0,1},{1,0},{2,3},{3,2},{4,5},{5,4},{6,7},{7,6},{8,9},{9,8},{10,11... | collective-permute-start | bytes 4616 | tf_op jit(solution)/shard_map/ppermute | solution.py:16
  9.0 44.1 %collective-permute-start = (f32[3,1]{1,0:T(4,128)}, f32[3,1]{1,0:T(4,128)S(1)}, u32[]{:S(2)}, u32[]{:S(2)}) collective-permute-start(f32[3,1]{1,0:T(4,128)} %bitcast.141), channel_id=1, source_target_pairs={{1,0},{2,1},{3,2},{4,3},{5,4},{6,5},{7,6},{8,7},{9,8},{10,9},{11,1... | collective-permute-start | bytes 44 | tf_op jit(solution)/shard_map/ppermute | solution.py:29
  54.0 3.7 %collective-permute-start.2 = (f32[3,256]{1,0:T(4,128)S(1)}, f32[3,256]{1,0:T(4,128)S(1)}, u32[]{:S(2)}, u32[]{:S(2)}) collective-permute-start(f32[3,256]{1,0:T(4,128)S(1)} %maximum_select_fusion.3), channel_id=1, source_target_pairs={{0,2},{1,3},{2,0},{3,1},{4,6},{5,7},{6,4},{7,5},{8,10},{9,11},{10,... | collective-permute-start | bytes 9224 | tf_op jit(solution)/shard_map/ppermute | solution.py:16
  57.7 3.7 %collective-permute-start.3 = (f32[3,512]{1,0:T(4,128)S(1)}, f32[3,512]{1,0:T(4,128)S(1)}, u32[]{:S(2)}, u32[]{:S(2)}) collective-permute-start(f32[3,512]{1,0:T(4,128)S(1)} %maximum_select_fusion.2), channel_id=1, source_target_pairs={{0,4},{1,5},{2,6},{3,7},{4,0},{5,1},{6,2},{7,3},{8,12},{9,13},{10,... | collective-permute-start | bytes 18440 | tf_op jit(solution)/shard_map/ppermute | solution.py:16
  61.3 4.6 %collective-permute-start.4 = (f32[3,1024]{1,0:T(4,128)S(1)}, f32[3,1024]{1,0:T(4,128)S(1)}, u32[]{:S(2)}, u32[]{:S(2)}) collective-permute-start(f32[3,1024]{1,0:T(4,128)S(1)} %maximum_select_fusion.1), channel_id=1, source_target_pairs={{0,8},{1,9},{2,10},{3,11},{4,12},{5,13},{6,14},{7,15},{8,0},{9,1},... | collective-permute-start | bytes 36872 | tf_op jit(solution)/shard_map/ppermute | solution.py:16
  66.8 0.7 copy-start.2
  66.8 0.7 copy-start.3
  81.9 3.4 %copy-start = (f32[1,128,2048]{2,1,0:T(8,128)S(1)}, f32[1,128,2048]{2,1,0:T(8,128)}, u32[]{:S(2)}) copy-start(f32[1,128,2048]{2,1,0:T(8,128)} %get-tuple-element.87) | copy-start | bytes 3145732
  85.4 4.4 %copy-start.1 = (f32[3]{0:T(128)S(1)}, f32[3]{0:T(128)}, u32[]{:S(2)}) copy-start(f32[3]{0:T(128)} %constant.15.clone) | copy-start | bytes 40
  90.5 2.1 %collective-permute-start.5 = (f32[3,1]{0,1:T(1,128)S(1)}, f32[3,1]{0,1:T(1,128)S(1)}, u32[]{:S(2)}, u32[]{:S(2)}) collective-permute-start(f32[3,1]{0,1:T(1,128)S(1)} %slice.108), channel_id=1, source_target_pairs={{0,1},{1,2},{2,3},{3,4},{4,5},{5,6},{6,7},{7,8},{8,9},{9,10},{10,1... | collective-permute-start | bytes 44 | tf_op jit(solution)/shard_map/ppermute | solution.py:29
Sparse Core Ops, SparseCore 0:
  90.7 50.2 reduce-scatter.1
